TPU v7x, 512 devices: a whole 4x4x16 slice. The times are simulated.
512 devices in a mesh: obs: 16 (over z), src: 32 (over x, y, core).
Axes of the slice: x: 4, y: 4, z: 16, core: 2. Of those that a mesh axis runs over, the one named last changes fastest.
Arguments:
- delay_near: bfloat16 [16384, 16384], P('src', 'obs'), may hold values from -0.09375 to 0.09375
- delay_far: bfloat16 [16384, 16384], P('src', 'obs'), may hold values from -0.046875 to 0.046875
- incident: bfloat16 [4, 16384, 192], P(None, 'src'), may hold values from -6 to 6
- current_prev: bfloat16 [16384, 192], P('obs'), may hold values from -0.8984375 to 0.8984375
- current_prev2: bfloat16 [16384, 192], P('obs'), may hold values from -0.8984375 to 0.8984375
Outputs:
- currents: bfloat16 [4, 16384, 192], P(None, 'obs')
All inputs are finite; a program needn't handle non-finite values.
Results may differ from a plain program's by a relative error of at most 0.003.
Values may be sent and summed in bfloat16 or wider, within the bound.
A program may use at most 64 MiB of HBM per device.

v0:
```python
import jax
import jax.numpy as jnp
from jax import lax
from jax.sharding import PartitionSpec as P

STEPS = 4


def split_up(x, dim, size):
    before, after = (x.shape[:dim], x.shape[dim + 1 :])
    return jnp.moveaxis(x.reshape(*before, size, -1, *after), dim, 0)


def sum_at_owner(x, axis, dim):
    size = lax.axis_size(axis)
    blocks = lax.all_to_all(split_up(x, dim, size), axis, 0, 0, tiled=True)
    return jnp.sum(blocks, axis=0)


def copy_for_each(x, axis):
    copies = jnp.broadcast_to(x, (lax.axis_size(axis), *x.shape))
    return lax.all_to_all(copies, axis, split_axis=0, concat_axis=0, tiled=True)


def joined_along(blocks, dim):
    shape = list(blocks.shape[1:])
    shape[dim] *= blocks.shape[0]
    return jnp.moveaxis(blocks, 0, dim).reshape(shape)


def gather_directly(x, axis, dim):
    blocks = copy_for_each(x, axis)
    return joined_along(blocks, dim)


def from_root(x, axis, root):
    return lax.dynamic_index_in_dim(lax.all_gather(x, axis), root, 0, keepdims=False)


def per_device(delay_near, delay_far, incident, current_prev, current_prev2):
    lagged = current_prev2
    latest = current_prev
    group_ratio = lax.axis_size("src") // lax.axis_size("obs")
    source_index = lax.axis_index("obs")
    share_rows = delay_near.shape[0] // lax.axis_size("obs")
    history = []
    for moment in range(STEPS):

        def partial_term(first_row, row_count, newer_rows=latest, older_rows=lagged):
            total = jnp.dot(delay_near, newer_rows, preferred_element_type=jnp.float32)
            return total + jnp.dot(delay_far, older_rows, preferred_element_type=jnp.float32)

        field_share = sum_at_owner(
            partial_term(jnp.int32(0), share_rows * lax.axis_size("obs")), "obs", 0
        )
        local_field = lax.dynamic_slice_in_dim(
            incident[moment], source_index * share_rows, share_rows, 0
        )
        law_piece = jnp.tanh(local_field.astype(jnp.float32) - field_share).astype(jnp.bfloat16)
        block_current = gather_directly(law_piece, "obs", 0)
        pieces = []
        for member in range(group_ratio):
            root_index = source_index * group_ratio + member
            pieces.append(from_root(block_current, "src", root_index))
        new_current = jnp.concatenate(pieces, axis=0)
        history.append(new_current)
        lagged = latest
        latest = new_current
    return jnp.stack(history)


def solution(mesh):
    in_specs = (
        P("src", "obs"),
        P("src", "obs"),
        P(None, "src", None),
        P("obs", None),
        P("obs", None),
    )
    out_specs = P(None, "obs", None)
    return jax.shard_map(
        per_device, mesh=mesh, in_specs=in_specs, out_specs=out_specs, check_vma=False
    )
```

profile of v0, /device:TPU:1, one launch (start us, length us, event | category | flops | bytes accessed | tf_op | source)
XLA Modules:
  0.0 535.0 jit_solution(11801956042533614111)
XLA Ops:
  6.5 0.0 copy-start
  6.5 0.0 copy-start.2
  6.5 0.0 copy-start.1
  6.5 1.2 copy-done
  7.8 1.5 fusion.21
  9.3 1.8 convolution_add_fusion.3
  11.1 1.0 copy.31
  12.1 15.7 %all-to-all-start = ((f32[16,32,192]{2,1,0:T(8,128)}), f32[16,32,192]{2,1,0:T(8,128)S(1)}, u32[]{:S(2)}, u32[]{:S(2)}) async-start(f32[16,32,192]{2,1,0:T(8,128)} %bitcast.1), calls=%async_computation | async-start | bytes 1048576 | tf_op jit(solution)/shard_map/all_to_all | solution.py:16
  27.8 0.0 all-gather.5.cloned.1.call-start
  27.9 2.1 fusion.20
  29.9 0.1 constant_dynamic-slice_fusion.3
  30.0 0.1 copy.43
  30.1 20.7 %all-to-all-done = f32[16,32,192]{2,1,0:T(8,128)S(1)} async-done(((f32[16,32,192]{2,1,0:T(8,128)}), f32[16,32,192]{2,1,0:T(8,128)S(1)}, u32[]{:S(2)}, u32[]{:S(2)}) %all-to-all-start) | async-done | bytes 393248 | tf_op jit(solution)/shard_map/all_to_all | solution.py:16
  50.9 26.0 %all_to_all.40 = bf16[16,32,192]{2,1,0:T(8,128)(2,1)S(1)} all-to-all(bf16[16,32,192]{2,1,0:T(8,128)(2,1)S(1)} %broadcast_in_dim.12), channel_id=1, replica_groups=mesh['obs'=16,'src'=32] {'obs'}, dimensions={0} | all-to-all | bytes 393216 | tf_op jit(solution)/shard_map/all_to_all | solution.py:22
  76.9 0.8 copy.32
  77.7 0.0 all-gather.5.cloned.1.call-update
  77.7 64.8 %all-gather.5.cloned.1.call-done = bf16[32,512,192]{1,2,0:T(8,128)(2,1)} async-done(((bf16[1,512,192]{1,2,0:T(8,128)(2,1)}), bf16[32,512,192]{1,2,0:T(8,128)(2,1)}) %all-gather.5.cloned.1.call-update) | async-done | bytes 6291472 | tf_op jit(solution)/shard_map/all_gather | solution.py:37
  142.5 1.0 dynamic-slice_bitcast_fusion.7
  143.5 0.5 convolution_bitcast_fusion
  144.0 0.0 copy-done.2
  144.1 0.0 copy-done.1
  144.1 0.5 convolution_add_fusion.2
  144.6 1.0 copy.34
  145.6 12.0 %all-to-all-start.2 = ((f32[16,32,192]{2,1,0:T(8,128)}), f32[16,32,192]{2,1,0:T(8,128)S(1)}, u32[]{:S(2)}, u32[]{:S(2)}) async-start(f32[16,32,192]{2,1,0:T(8,128)} %bitcast.8), calls=%async_computation.2 | async-start | bytes 1048576 | tf_op jit(solution)/shard_map/all_to_all | solution.py:16
  157.6 0.0 all-gather.7.cloned.1.call-start
  157.6 0.9 constant_dynamic-slice_fusion.2
  158.5 0.1 copy.45
  158.6 21.6 %all-to-all-done.2 = f32[16,32,192]{2,1,0:T(8,128)S(1)} async-done(((f32[16,32,192]{2,1,0:T(8,128)}), f32[16,32,192]{2,1,0:T(8,128)S(1)}, u32[]{:S(2)}, u32[]{:S(2)}) %all-to-all-start.2) | async-done | bytes 393248 | tf_op jit(solution)/shard_map/all_to_all | solution.py:16
  180.3 26.5 %all_to_all.41 = bf16[16,32,192]{2,1,0:T(8,128)(2,1)S(1)} all-to-all(bf16[16,32,192]{2,1,0:T(8,128)(2,1)S(1)} %broadcast_in_dim.13), channel_id=1, replica_groups=mesh['obs'=16,'src'=32] {'obs'}, dimensions={0} | all-to-all | bytes 393216 | tf_op jit(solution)/shard_map/all_to_all | solution.py:22
  206.9 0.8 copy.35
  207.7 0.0 all-gather.7.cloned.1.call-update
  207.7 62.1 %all-gather.7.cloned.1.call-done = bf16[32,512,192]{1,2,0:T(8,128)(2,1)} async-done(((bf16[1,512,192]{1,2,0:T(8,128)(2,1)}), bf16[32,512,192]{1,2,0:T(8,128)(2,1)}) %all-gather.7.cloned.1.call-update) | async-done | bytes 6291472 | tf_op jit(solution)/shard_map/all_gather | solution.py:37
  269.8 1.0 dynamic-slice_bitcast_fusion.5
  270.8 0.5 fusion.4
  271.3 0.5 fusion.1
  271.8 1.0 copy.37
  272.8 12.0 %all-to-all-start.4 = ((f32[16,32,192]{2,1,0:T(8,128)}), f32[16,32,192]{2,1,0:T(8,128)S(1)}, u32[]{:S(2)}, u32[]{:S(2)}) async-start(f32[16,32,192]{2,1,0:T(8,128)} %bitcast.61), calls=%async_computation.4 | async-start | bytes 1048576 | tf_op jit(solution)/shard_map/all_to_all | solution.py:16
  284.8 0.0 all-gather.9.cloned.1.call-start
  284.9 0.9 constant_dynamic-slice_fusion.1
  285.8 0.1 copy.47
  285.8 21.6 %all-to-all-done.4 = f32[16,32,192]{2,1,0:T(8,128)S(1)} async-done(((f32[16,32,192]{2,1,0:T(8,128)}), f32[16,32,192]{2,1,0:T(8,128)S(1)}, u32[]{:S(2)}, u32[]{:S(2)}) %all-to-all-start.4) | async-done | bytes 393248 | tf_op jit(solution)/shard_map/all_to_all | solution.py:16
  307.6 26.5 %all_to_all.42 = bf16[16,32,192]{2,1,0:T(8,128)(2,1)S(1)} all-to-all(bf16[16,32,192]{2,1,0:T(8,128)(2,1)S(1)} %broadcast_in_dim.14), channel_id=1, replica_groups=mesh['obs'=16,'src'=32] {'obs'}, dimensions={0} | all-to-all | bytes 393216 | tf_op jit(solution)/shard_map/all_to_all | solution.py:22
  334.1 0.8 copy.38
  334.9 0.0 all-gather.9.cloned.1.call-update
  334.9 62.1 %all-gather.9.cloned.1.call-done = bf16[32,512,192]{1,2,0:T(8,128)(2,1)} async-done(((bf16[1,512,192]{1,2,0:T(8,128)(2,1)}), bf16[32,512,192]{1,2,0:T(8,128)(2,1)}) %all-gather.9.cloned.1.call-update) | async-done | bytes 6291472 | tf_op jit(solution)/shard_map/all_gather | solution.py:37
  397.0 1.0 dynamic-slice_bitcast_fusion.3
  398.1 0.5 fusion.2
  398.6 1.3 fusion
  399.8 2.0 copy.40
  401.8 12.0 %all-to-all-start.6 = ((f32[16,32,192]{2,1,0:T(8,128)}), f32[16,32,192]{2,1,0:T(8,128)S(1)}, u32[]{:S(2)}, u32[]{:S(2)}) async-start(f32[16,32,192]{2,1,0:T(8,128)} %bitcast.22), calls=%async_computation.6 | async-start | bytes 1048576 | tf_op jit(solution)/shard_map/all_to_all | solution.py:16
  413.8 0.0 all-gather.11.cloned.1.call-start
  413.9 0.9 constant_dynamic-slice_fusion
  414.8 0.1 copy.49
  414.8 21.6 %all-to-all-done.6 = f32[16,32,192]{2,1,0:T(8,128)S(1)} async-done(((f32[16,32,192]{2,1,0:T(8,128)}), f32[16,32,192]{2,1,0:T(8,128)S(1)}, u32[]{:S(2)}, u32[]{:S(2)}) %all-to-all-start.6) | async-done | bytes 393248 | tf_op jit(solution)/shard_map/all_to_all | solution.py:16
  436.6 26.5 %all_to_all.43 = bf16[16,32,192]{2,1,0:T(8,128)(2,1)S(1)} all-to-all(bf16[16,32,192]{2,1,0:T(8,128)(2,1)S(1)} %broadcast_in_dim.15), channel_id=1, replica_groups=mesh['obs'=16,'src'=32] {'obs'}, dimensions={0} | all-to-all | bytes 393216 | tf_op jit(solution)/shard_map/all_to_all | solution.py:22
  463.1 0.8 copy.41
  463.9 0.0 all-gather.11.cloned.1.call-update
  464.1 61.9 %all-gather.11.cloned.1.call-done = bf16[32,512,192]{1,2,0:T(8,128)(2,1)} async-done(((bf16[1,512,192]{1,2,0:T(8,128)(2,1)}), bf16[32,512,192]{1,2,0:T(8,128)(2,1)}) %all-gather.11.cloned.1.call-update) | async-done | bytes 6291472 | tf_op jit(solution)/shard_map/all_gather | solution.py:37
  526.0 1.0 dynamic-slice_bitcast_fusion.1
  527.1 1.3 pad_maximum_fusion
  (16 shorter events, 0.5 us)
Async XLA Ops:
  6.5 1.2 copy-start
  6.5 137.5 %copy-start.2 = (bf16[1024,192]{0,1:T(8,128)(2,1)S(1)}, bf16[1024,192]{0,1:T(8,128)(2,1)}, u32[]{:S(2)}) copy-start(bf16[1024,192]{0,1:T(8,128)(2,1)} %param.8) | copy-start | bytes 1179652
  6.5 137.5 %copy-start.1 = (bf16[512,1024]{1,0:T(8,128)(2,1)S(1)}, bf16[512,1024]{1,0:T(8,128)(2,1)}, u32[]{:S(2)}) copy-start(bf16[512,1024]{1,0:T(8,128)(2,1)} %param.6) | copy-start | bytes 3145732
  12.1 38.7 %all-to-all-start = ((f32[16,32,192]{2,1,0:T(8,128)}), f32[16,32,192]{2,1,0:T(8,128)S(1)}, u32[]{:S(2)}, u32[]{:S(2)}) async-start(f32[16,32,192]{2,1,0:T(8,128)} %bitcast.1), calls=%async_computation | async-start | bytes 1048576 | tf_op jit(solution)/shard_map/all_to_all | solution.py:16
  27.8 114.7 %all-gather.5.cloned.1.call-start = ((), (), s32[]{:S(2)}) async-start(), calls=%async_computation.8 | async-start | bytes 6488064 | tf_op jit(solution)/shard_map/all_gather | solution.py:37
  145.6 34.7 %all-to-all-start.2 = ((f32[16,32,192]{2,1,0:T(8,128)}), f32[16,32,192]{2,1,0:T(8,128)S(1)}, u32[]{:S(2)}, u32[]{:S(2)}) async-start(f32[16,32,192]{2,1,0:T(8,128)} %bitcast.8), calls=%async_computation.2 | async-start | bytes 1048576 | tf_op jit(solution)/shard_map/all_to_all | solution.py:16
  157.6 112.2 %all-gather.7.cloned.1.call-start = ((), (), s32[]{:S(2)}) async-start(), calls=%async_computation.9 | async-start | bytes 6488064 | tf_op jit(solution)/shard_map/all_gather | solution.py:37
  272.8 34.6 %all-to-all-start.4 = ((f32[16,32,192]{2,1,0:T(8,128)}), f32[16,32,192]{2,1,0:T(8,128)S(1)}, u32[]{:S(2)}, u32[]{:S(2)}) async-start(f32[16,32,192]{2,1,0:T(8,128)} %bitcast.61), calls=%async_computation.4 | async-start | bytes 1048576 | tf_op jit(solution)/shard_map/all_to_all | solution.py:16
  284.8 112.2 %all-gather.9.cloned.1.call-start = ((), (), s32[]{:S(2)}) async-start(), calls=%async_computation.10 | async-start | bytes 6488064 | tf_op jit(solution)/shard_map/all_gather | solution.py:37
  401.8 34.6 %all-to-all-start.6 = ((f32[16,32,192]{2,1,0:T(8,128)}), f32[16,32,192]{2,1,0:T(8,128)S(1)}, u32[]{:S(2)}, u32[]{:S(2)}) async-start(f32[16,32,192]{2,1,0:T(8,128)} %bitcast.22), calls=%async_computation.6 | async-start | bytes 1048576 | tf_op jit(solution)/shard_map/all_to_all | solution.py:16
  413.8 112.2 %all-gather.11.cloned.1.call-start = ((), (), s32[]{:S(2)}) async-start(), calls=%async_computation.11 | async-start | bytes 6488064 | tf_op jit(solution)/shard_map/all_gather | solution.py:37
Sparse Core Ops, SparseCore 0:
  77.8 64.5 all-gather.4
  207.8 61.9 all-gather.6
  335.1 61.9 all-gather.8
  464.1 61.9 all-gather.10
where the time goes:
time: 536 us; the launch traced here: 535 us
  waiting for transfers between devices  337 us (63%)
  blocking collectives  106 us (20%)
  starting transfers between devices  51.9 us (10%)
  local copies, waits for them, and re-layouts  18.7 us (3%)
  between operations  13.4 us (2%)
  matrix products  7.09 us (1%)
    all_gather x4, waiting for transfers between devices, from_root(): lax.all_gather(x, axis)  251 us
    all_to_all x4, blocking collectives, copy_for_each(): return lax.all_to_all(copies, axis, split_axis=0, concat_axis=0, tiled=True)  106 us
    all_to_all x4, waiting for transfers between devices, sum_at_owner(): blocks = lax.all_to_all(split_up(x, dim, size), axis, 0, 0, tiled=True)  85.6 us
    all_to_all x4, starting transfers between devices, sum_at_owner(): blocks = lax.all_to_all(split_up(x, dim, size), axis, 0, 0, tiled=True)  51.8 us
  transfers between devices with their start and end apart: 8, of which 8 were waited for; matrix products, arithmetic and copies ran while one was open for 1% of the time, Pallas kernels for 0%

commit v1 on v0

v1 whole, which is shorter than its diff:
```python
import functools
import math

import jax
import jax.numpy as jnp
from jax import lax
from jax.experimental import pallas as pl
from jax.experimental.pallas import tpu as pltpu
from jax.sharding import PartitionSpec as P

BATCHES = 4
GROUP = 2
WIRE = jnp.float32
MESH = pl.DeviceIdType.MESH


def both(*conds):
    return functools.reduce(jnp.logical_and, conds)


def kernel(
    steps, nz, side, near_ref, far_ref, inc_ref, prev_ref, prev2_ref, out_ref,
    cur, acc, lag, snd, got, inct, z_send, z_recv, b_send, b_recv, out_sem,
):
    nb, rb, m = acc.shape
    z = lax.axis_index("obs")
    src = lax.axis_index("src")
    core = lax.rem(src, 2)
    chip = src // 2
    x, y = chip // side, lax.rem(chip, side)

    rel = lax.rem(z - chip + nz, nz)
    upper = rel <= nz // 2
    dist = jnp.where(upper, rel, nz - rel)
    arm = jnp.where(upper, nz // 2, nz - nz // 2 - 1)
    is_root = rel == 0
    hop = jnp.where(lax.rem(dist, GROUP) == 0, GROUP, lax.rem(dist, GROUP))
    parent_z = lax.rem(jnp.where(upper, z - hop, z + hop) + nz, nz)
    parent_slot = hop - 1 + jnp.where(both(jnp.logical_not(upper), dist == hop), GROUP, 0)
    is_leaf = both(jnp.logical_not(is_root), (lax.rem(dist, GROUP) != 0) | (dist + 1 > arm))
    is_joint = both(jnp.logical_not(is_root), jnp.logical_not(is_leaf))

    rx, ry = z // side, lax.rem(z, side)
    dx = lax.rem(x - rx + side, side)
    dy = lax.rem(y - ry + side, side)
    is_source = both(dx == 0, dy == 0)
    sibling = (z, chip * 2 + 1 - core)

    def in_plane(kx, ky):
        tx = lax.rem(x + kx, side)
        ty = lax.rem(y + ky, side)
        return (z, (tx * side + ty) * 2 + core)

    peers = [in_plane(k, 0) for k in range(1, side)]
    peers += [in_plane(0, k) for k in range(1, side)]
    peers += [sibling]
    reach = sorted({k % nz for k in range(-GROUP, GROUP + 1)} - {0})
    peers += [(lax.rem(z + k, nz), src) for k in reach]
    barrier = pltpu.get_barrier_semaphore()
    for peer in peers:
        pl.semaphore_signal(barrier, inc=1, device_id=peer, device_id_type=MESH)

    for index, ref in ((0, prev2_ref), (1, prev_ref)):
        whole = ref[...].astype(jnp.float32).T.astype(jnp.bfloat16)
        for b in range(nb):
            for h in range(2):
                cur[index, b, h] = whole[b * rb : (b + 1) * rb, h * m : (h + 1) * m]

    def dot(rows, ref, half):
        cols = pl.ds(pl.multiple_of(half * m, m), m)
        return lax.dot_general(
            rows, ref[:, cols], (((1,), (1,)), ((), ())), preferred_element_type=jnp.float32
        )

    def lagged(index, b):
        lag[b] = dot(cur[index, b, 0], far_ref, 0) + dot(cur[index, b, 1], far_ref, 1)

    for b in range(nb):
        lagged(0, b)

    @pl.when(is_root)
    def _():
        for t in range(steps):
            inct[t] = inc_ref[t].astype(jnp.float32).T.reshape(nb, rb, m)

    pl.semaphore_wait(barrier, len(peers))

    def up(t, b):
        return pltpu.make_async_remote_copy(
            src_ref=snd.at[t, b], dst_ref=got.at[t, b, parent_slot],
            send_sem=z_send.at[t, b], recv_sem=z_recv.at[t, b, parent_slot],
            device_id=(parent_z, src), device_id_type=MESH,
        )

    def down(t, b, which, device):
        return pltpu.make_async_remote_copy(
            src_ref=cur.at[t + 2, b, core], dst_ref=cur.at[t + 2, b, core],
            send_sem=b_send.at[t, b, which], recv_sem=b_recv.at[t, b, core],
            device_id=device, device_id_type=MESH,
        )

    def wait_block(t, b, half):
        pltpu.make_async_remote_copy(
            src_ref=cur.at[t + 2, b, half], dst_ref=cur.at[t + 2, b, half],
            send_sem=b_send.at[t, b, 0], recv_sem=b_recv.at[t, b, half],
            device_id=sibling, device_id_type=MESH,
        ).wait_recv()

    def second_level(b):
        odd = lax.rem(b, 2)
        across = jnp.where(odd == 0, dy, dx) == 0
        return across, [in_plane(k * odd, k * (1 - odd)) for k in range(1, side)]

    def first_level(b):
        odd = lax.rem(b, 2)
        return [in_plane(k * (1 - odd), k * odd) for k in range(1, side)]

    def relay(t, b, start):
        across, targets = second_level(b)

        @pl.when(across)
        def _():
            for k, target in enumerate(targets):
                copy = down(t, b, 1 + k, target)
                copy.start() if start else copy.wait_send()

        copy = down(t, b, 0, sibling)
        copy.start() if start else copy.wait_send()

    def source(t, b, start):
        for k, target in enumerate(first_level(b)):
            copy = down(t, b, side + k, target)
            copy.start() if start else copy.wait_send()

    def take_own(t, b):
        @pl.when(jnp.logical_not(is_source))
        def _():
            wait_block(t, b, core)
            relay(t, b, True)

    def ahead(t, b):
        @pl.when(t > 0)
        def _():
            take_own(t - 1, b)

        total = lag[b] + dot(cur[t + 1, b, core], near_ref, core)

        @pl.when(t > 0)
        def _():
            wait_block(t - 1, b, 1 - core)

        total = total + dot(cur[t + 1, b, 1 - core], near_ref, 1 - core)

        @pl.when(is_leaf)
        def _():
            snd[t, b] = total.astype(WIRE)
            up(t, b).start()

        @pl.when(jnp.logical_not(is_leaf))
        def _():
            acc[b] = total

    def wait_part(t, b, slot):
        pltpu.make_async_remote_copy(
            src_ref=snd.at[t, b], dst_ref=got.at[t, b, slot],
            send_sem=z_send.at[t, b], recv_sem=z_recv.at[t, b, slot],
            device_id=(parent_z, src), device_id_type=MESH,
        ).wait_recv()

    def behind(t, b):
        @pl.when(is_joint)
        def _():
            for k in range(GROUP):
                @pl.when(dist + k + 1 <= arm)
                def _():
                    wait_part(t, b, k)
                    acc[b] += got[t, b, k].astype(jnp.float32)

            snd[t, b] = acc[b].astype(WIRE)
            up(t, b).start()

        @pl.when(is_root)
        def _():
            total = acc[b]
            for k in range(GROUP):
                for lower, length in ((0, nz // 2), (1, nz - nz // 2 - 1)):
                    if k + 1 <= length:
                        wait_part(t, b, k + GROUP * lower)
                        total = total + got[t, b, k + GROUP * lower].astype(jnp.float32)
            cur[t + 2, b, core] = jnp.tanh(inct[t, b] - total).astype(jnp.bfloat16)
            source(t, b, True)
            relay(t, b, True)

    skew = jnp.where(is_leaf, 0, jnp.where(arm - dist <= 2, 1, nb))

    def out_copy(t):
        return pltpu.make_async_copy(cur.at[t + 2], out_ref.at[t], out_sem.at[t])

    def step(t, carry):
        def turn(j, carry):
            @pl.when(j < nb)
            def _():
                ahead(t, j)

            @pl.when(both(j >= skew, j - skew < nb))
            def _():
                behind(t, j - skew)

            return carry

        lax.fori_loop(0, 2 * nb, turn, 0)

        @pl.when(t > 0)
        def _():
            out_copy(t - 1).start()

        @pl.when(t < steps - 1)
        def _():
            def refill(b, carry):
                lagged(t + 1, b)
                return carry

            lax.fori_loop(0, nb, refill, 0)

        return carry

    lax.fori_loop(0, steps, step, 0)

    def finish(b, carry):
        take_own(steps - 1, b)
        wait_block(steps - 1, b, 1 - core)
        return carry

    lax.fori_loop(0, nb, finish, 0)
    out_copy(steps - 1).start()

    def drain(i, carry):
        t, b = i // nb, lax.rem(i, nb)
        relay(t, b, False)

        @pl.when(is_source)
        def _():
            source(t, b, False)

        @pl.when(jnp.logical_not(is_root))
        def _():
            up(t, b).wait_send()

        return carry

    lax.fori_loop(0, steps * nb, drain, 0)
    for t in range(steps):
        out_copy(t).wait()


def per_device(delay_near, delay_far, incident, current_prev, current_prev2):
    steps, m, r = incident.shape
    nz = lax.axis_size("obs")
    side = math.isqrt(lax.axis_size("src") // 2)
    nb = BATCHES
    rb = r // nb
    vmem = pl.BlockSpec(memory_space=pltpu.VMEM)
    blocks = pl.pallas_call(
        functools.partial(kernel, steps, nz, side),
        out_shape=jax.ShapeDtypeStruct((steps, nb, 2, rb, m), jnp.bfloat16),
        in_specs=[vmem] * 5,
        out_specs=pl.BlockSpec(memory_space=pl.ANY),
        scratch_shapes=[
            pltpu.VMEM((steps + 2, nb, 2, rb, m), jnp.bfloat16),
            pltpu.VMEM((nb, rb, m), jnp.float32),
            pltpu.VMEM((nb, rb, m), jnp.float32),
            pltpu.VMEM((steps, nb, rb, m), WIRE),
            pltpu.VMEM((steps, nb, 2 * GROUP, rb, m), WIRE),
            pltpu.VMEM((steps, nb, rb, m), jnp.float32),
            pltpu.SemaphoreType.DMA((steps, nb)),
            pltpu.SemaphoreType.DMA((steps, nb, 2 * GROUP)),
            pltpu.SemaphoreType.DMA((steps, nb, 2 * side)),
            pltpu.SemaphoreType.DMA((steps, nb, 2)),
            pltpu.SemaphoreType.DMA((steps,)),
        ],
        compiler_params=pltpu.CompilerParams(collective_id=0, has_side_effects=True),
    )(delay_near, delay_far, incident, current_prev, current_prev2)
    return blocks.transpose(0, 2, 4, 1, 3).reshape(steps, 2 * m, r)


def solution(mesh):
    in_specs = (
        P("src", "obs"),
        P("src", "obs"),
        P(None, "src", None),
        P("obs", None),
        P("obs", None),
    )
    out_specs = P(None, "obs", None)
    return jax.shard_map(
        per_device, mesh=mesh, in_specs=in_specs, out_specs=out_specs, check_vma=False
    )
```

time: 536 us -> 172 us (0.32)
  the two profiles are of different devices: /device:TPU:1 before, /device:TPU:37 now
where the time goes in v1:
time: 172 us
  Pallas kernels  161 us (94%)
  local copies, waits for them, and re-layouts  10.7 us (6%)
    pallas_call x1, Pallas kernels, per_device(): pl.pallas_call(functools.partial(kernel, steps, nz, side), out_shape=jax....  161 us
    unnamed x5, local copies, waits for them, and re-layouts  5.37 us

profile of v1, /device:TPU:37, one launch (start us, length us, event | category | flops | bytes accessed | tf_op | source)
XLA Modules:
  0.0 171.5 jit_solution(8667200965465672276)
XLA Ops:
  0.0 0.0 copy-start
  0.0 2.1 %copy.10.prev_ref = bf16[1024,192]{1,0:T(8,128)(2,1)} copy(bf16[1024,192]{0,1:T(8,128)(2,1)} %param.8) | data formatting | bytes 786432 | tf_op args[3]
  2.1 2.0 %copy.11.prev2_ref = bf16[1024,192]{1,0:T(8,128)(2,1)} copy(bf16[1024,192]{0,1:T(8,128)(2,1)} %param.9) | data formatting | bytes 786432 | tf_op args[4]
  4.1 0.0 copy-done
  4.1 1.3 copy.9.inc_ref
  5.4 160.8 %shard_map.55 = bf16[4,4,2,48,512]{4,3,2,1,0:T(8,128)(2,1)} custom-call(bf16[512,1024]{1,0:T(8,128)(2,1)} %near_ref.1, bf16[512,1024]{1,0:T(8,128)(2,1)} %far_ref.1, bf16[4,512,192]{2,1,0:T(8,128)(2,1)} %copy.9.inc_ref, bf16[1024,192]{1,0:T(8,128)(2,1)} %copy.10.prev_ref, bf16[1024,192]{1,0:T(8,128)(2,1)} %copy.11.prev2_ref), custom_call_target="tpu_custom_call" | custom-call | tf_op jit(solution)/shard_map/pallas_call | solution.py:263
  166.2 3.0 %copy.12 = bf16[4,2,512,4,48]{2,1,4,3,0:T(2,128)(2,1)S(1)} copy(bf16[4,2,512,4,48]{2,4,1,3,0:T(8,128)(2,1)} %bitcast.3) | data formatting | bytes 3145728 | tf_op jit(solution)/shard_map/transpose | solution.py:283
  169.2 2.3 %reshape.3 = bf16[4,1024,192]{1,2,0:T(8,128)(2,1)} reshape(bf16[4,2,512,4,48]{2,1,4,3,0:T(2,128)(2,1)S(1)} %copy.12) | data formatting | bytes 3145728 | tf_op jit(solution)/shard_map/reshape | solution.py:283
Async XLA Ops:
  0.0 4.1 %copy-start = (bf16[4,512,192]{1,2,0:T(8,128)(2,1)S(1)}, bf16[4,512,192]{1,2,0:T(8,128)(2,1)}, u32[]{:S(2)}) copy-start(bf16[4,512,192]{1,2,0:T(8,128)(2,1)} %param.7) | copy-start | bytes 2359300

commit v2 on v1

--- a/solution.py
+++ b/solution.py
@@ -8,9 +8,10 @@
 from jax.experimental.pallas import tpu as pltpu
 from jax.sharding import PartitionSpec as P
 
-BATCHES = 4
-GROUP = 2
-WIRE = jnp.float32
+BATCHES = 12
+TOGETHER = 2
+NEAR, FAR = 2, 6
+SKEW = 3
 MESH = pl.DeviceIdType.MESH
 
 
@@ -18,9 +19,19 @@
     return functools.reduce(jnp.logical_and, conds)
 
 
+def coded(v):
+    return (v * v * v * jnp.abs(v)).astype(jnp.bfloat16)
+
+
+def decoded(c):
+    c = c.astype(jnp.float32)
+    size = lax.rsqrt(lax.rsqrt(jnp.abs(c) + 1e-36))
+    return jnp.where(c < 0, -size, size)
+
+
 def kernel(
     steps, nz, side, near_ref, far_ref, inc_ref, prev_ref, prev2_ref, out_ref,
-    cur, acc, lag, snd, got, inct, z_send, z_recv, b_send, b_recv, out_sem,
+    near, far, inct, cur, acc, lag, snd, got, z_send, z_recv, b_send, b_recv, in_sem, out_sem,
 ):
     nb, rb, m = acc.shape
     z = lax.axis_index("obs")
@@ -34,11 +45,15 @@
     dist = jnp.where(upper, rel, nz - rel)
     arm = jnp.where(upper, nz // 2, nz - nz // 2 - 1)
     is_root = rel == 0
-    hop = jnp.where(lax.rem(dist, GROUP) == 0, GROUP, lax.rem(dist, GROUP))
+    home = jnp.where(dist <= NEAR + 1, NEAR, FAR)
+    apart = dist - home
+    is_joint = both(jnp.logical_not(is_root), apart == 0)
+    is_leaf = both(jnp.logical_not(is_root), apart != 0)
+    to_root = (apart == 0) | (home > arm)
+    hop = jnp.where(to_root, dist, apart)
     parent_z = lax.rem(jnp.where(upper, z - hop, z + hop) + nz, nz)
-    parent_slot = hop - 1 + jnp.where(both(jnp.logical_not(upper), dist == hop), GROUP, 0)
-    is_leaf = both(jnp.logical_not(is_root), (lax.rem(dist, GROUP) != 0) | (dist + 1 > arm))
-    is_joint = both(jnp.logical_not(is_root), jnp.logical_not(is_leaf))
+    root_slot = jnp.where(home == FAR, 0, 1) + jnp.where(upper, 0, 2)
+    parent_slot = jnp.where(to_root, root_slot, jnp.where(apart > 0, 2 - apart, 1 - apart))
 
     rx, ry = z // side, lax.rem(z, side)
     dx = lax.rem(x - rx + side, side)
@@ -54,34 +69,48 @@
     peers = [in_plane(k, 0) for k in range(1, side)]
     peers += [in_plane(0, k) for k in range(1, side)]
     peers += [sibling]
-    reach = sorted({k % nz for k in range(-GROUP, GROUP + 1)} - {0})
+    reach = sorted({k % nz for k in (-FAR, -2, -1, 1, 2, FAR)} - {0})
     peers += [(lax.rem(z + k, nz), src) for k in reach]
     barrier = pltpu.get_barrier_semaphore()
     for peer in peers:
         pl.semaphore_signal(barrier, inc=1, device_id=peer, device_id_type=MESH)
 
-    for index, ref in ((0, prev2_ref), (1, prev_ref)):
-        whole = ref[...].astype(jnp.float32).T.astype(jnp.bfloat16)
-        for b in range(nb):
-            for h in range(2):
-                cur[index, b, h] = whole[b * rb : (b + 1) * rb, h * m : (h + 1) * m]
-
-    def dot(rows, ref, half):
+    def halves(ref, index):
+        return [(ref.at[:, :, h * m : (h + 1) * m], cur.at[index, :, h]) for h in range(2)]
+
+    loads = [(far_ref, far), *halves(prev2_ref, 0), (near_ref, near), *halves(prev_ref, 1)]
+    loads = [pltpu.make_async_copy(*pair, in_sem.at[i]) for i, pair in enumerate(loads)]
+    inc_load = pltpu.make_async_copy(inc_ref, inct, in_sem.at[6])
+    for load in loads:
+        load.start()
+
+    @pl.when(is_root)
+    def _():
+        inc_load.start()
+
+    k = TOGETHER
+
+    def dot(index, group, ref, half):
+        rows = cur[index, pl.ds(group * k, k), half].reshape(k * rb, m)
         cols = pl.ds(pl.multiple_of(half * m, m), m)
-        return lax.dot_general(
+        field = lax.dot_general(
             rows, ref[:, cols], (((1,), (1,)), ((), ())), preferred_element_type=jnp.float32
         )
-
-    def lagged(index, b):
-        lag[b] = dot(cur[index, b, 0], far_ref, 0) + dot(cur[index, b, 1], far_ref, 1)
-
-    for b in range(nb):
-        lagged(0, b)
+        return field.reshape(k, rb, m)
+
+    def lagged(index, group):
+        lag[pl.ds(group * k, k)] = dot(index, group, far, 0) + dot(index, group, far, 1)
+
+    for load in loads[:3]:
+        load.wait()
+    for group in range(nb // k):
+        lagged(0, group)
+    for load in loads[3:]:
+        load.wait()
 
     @pl.when(is_root)
     def _():
-        for t in range(steps):
-            inct[t] = inc_ref[t].astype(jnp.float32).T.reshape(nb, rb, m)
+        inc_load.wait()
 
     pl.semaphore_wait(barrier, len(peers))
 
@@ -143,22 +172,30 @@
         def _():
             take_own(t - 1, b)
 
-        total = lag[b] + dot(cur[t + 1, b, core], near_ref, core)
+        @pl.when(lax.rem(b, k) == k - 1)
+        def _():
+            multiply(t, b // k)
+
+    def multiply(t, group):
+        mine = pl.ds(group * k, k)
+        total = lag[mine] + dot(t + 1, group, near, core)
 
         @pl.when(t > 0)
         def _():
-            wait_block(t - 1, b, 1 - core)
-
-        total = total + dot(cur[t + 1, b, 1 - core], near_ref, 1 - core)
+            for i in range(k):
+                wait_block(t - 1, group * k + i, 1 - core)
+
+        total = total + dot(t + 1, group, near, 1 - core)
 
         @pl.when(is_leaf)
         def _():
-            snd[t, b] = total.astype(WIRE)
-            up(t, b).start()
+            snd[t, mine] = coded(total)
+            for i in range(k):
+                up(t, group * k + i).start()
 
         @pl.when(jnp.logical_not(is_leaf))
         def _():
-            acc[b] = total
+            acc[mine] = total
 
     def wait_part(t, b, slot):
         pltpu.make_async_remote_copy(
@@ -170,31 +207,37 @@
     def behind(t, b):
         @pl.when(is_joint)
         def _():
-            for k in range(GROUP):
-                @pl.when(dist + k + 1 <= arm)
-                def _():
-                    wait_part(t, b, k)
-                    acc[b] += got[t, b, k].astype(jnp.float32)
-
-            snd[t, b] = acc[b].astype(WIRE)
+            for slot, offset in enumerate((2, 1, -1, -2)):
+                child = dist + offset
+
+                @pl.when(both(child <= arm, (home == FAR) | (abs(offset) == 1)))
+                def _(slot=slot):
+                    wait_part(t, b, slot)
+                    acc[b] += decoded(got[t, b, slot])
+
+            snd[t, b] = coded(acc[b])
             up(t, b).start()
 
         @pl.when(is_root)
         def _():
             total = acc[b]
-            for k in range(GROUP):
-                for lower, length in ((0, nz // 2), (1, nz - nz // 2 - 1)):
-                    if k + 1 <= length:
-                        wait_part(t, b, k + GROUP * lower)
-                        total = total + got[t, b, k + GROUP * lower].astype(jnp.float32)
-            cur[t + 2, b, core] = jnp.tanh(inct[t, b] - total).astype(jnp.bfloat16)
+            for slot, least in ((1, 1), (0, FAR), (3, 1), (2, FAR)):
+                if least <= (nz // 2 if slot < 2 else nz - nz // 2 - 1):
+                    wait_part(t, b, slot)
+                    total = total + decoded(got[t, b, slot])
+            cur[t + 2, b, core] = jnp.tanh(inct[t, b].astype(jnp.float32) - total).astype(jnp.bfloat16)
             source(t, b, True)
             relay(t, b, True)
 
-    skew = jnp.where(is_leaf, 0, jnp.where(arm - dist <= 2, 1, nb))
-
-    def out_copy(t):
-        return pltpu.make_async_copy(cur.at[t + 2], out_ref.at[t], out_sem.at[t])
+    skew = jnp.where(is_leaf, 0, jnp.where(is_root, nb, SKEW))
+
+    def out_copies(t):
+        return [
+            pltpu.make_async_copy(
+                cur.at[t + 2, :, h], out_ref.at[t, :, :, h * m : (h + 1) * m], out_sem.at[t, h]
+            )
+            for h in range(2)
+        ]
 
     def step(t, carry):
         def turn(j, carry):
@@ -212,15 +255,16 @@
 
         @pl.when(t > 0)
         def _():
-            out_copy(t - 1).start()
+            for copy in out_copies(t - 1):
+                copy.start()
 
         @pl.when(t < steps - 1)
         def _():
-            def refill(b, carry):
-                lagged(t + 1, b)
+            def refill(group, carry):
+                lagged(t + 1, group)
                 return carry
 
-            lax.fori_loop(0, nb, refill, 0)
+            lax.fori_loop(0, nb // k, refill, 0)
 
         return carry
 
@@ -232,7 +276,8 @@
         return carry
 
     lax.fori_loop(0, nb, finish, 0)
-    out_copy(steps - 1).start()
+    for copy in out_copies(steps - 1):
+        copy.start()
 
     def drain(i, carry):
         t, b = i // nb, lax.rem(i, nb)
@@ -250,7 +295,8 @@
 
     lax.fori_loop(0, steps * nb, drain, 0)
     for t in range(steps):
-        out_copy(t).wait()
+        for copy in out_copies(t):
+            copy.wait()
 
 
 def per_device(delay_near, delay_far, incident, current_prev, current_prev2):
@@ -259,28 +305,37 @@
     side = math.isqrt(lax.axis_size("src") // 2)
     nb = BATCHES
     rb = r // nb
-    vmem = pl.BlockSpec(memory_space=pltpu.VMEM)
+    rows = (nb, rb, 2 * m)
     blocks = pl.pallas_call(
         functools.partial(kernel, steps, nz, side),
-        out_shape=jax.ShapeDtypeStruct((steps, nb, 2, rb, m), jnp.bfloat16),
-        in_specs=[vmem] * 5,
+        out_shape=jax.ShapeDtypeStruct((steps, *rows), jnp.bfloat16),
+        in_specs=[pl.BlockSpec(memory_space=pl.ANY)] * 5,
         out_specs=pl.BlockSpec(memory_space=pl.ANY),
         scratch_shapes=[
+            pltpu.VMEM((m, 2 * m), jnp.bfloat16),
+            pltpu.VMEM((m, 2 * m), jnp.bfloat16),
+            pltpu.VMEM((steps, nb, rb, m), jnp.bfloat16),
             pltpu.VMEM((steps + 2, nb, 2, rb, m), jnp.bfloat16),
             pltpu.VMEM((nb, rb, m), jnp.float32),
             pltpu.VMEM((nb, rb, m), jnp.float32),
-            pltpu.VMEM((steps, nb, rb, m), WIRE),
-            pltpu.VMEM((steps, nb, 2 * GROUP, rb, m), WIRE),
-            pltpu.VMEM((steps, nb, rb, m), jnp.float32),
+            pltpu.VMEM((steps, nb, rb, m), jnp.bfloat16),
+            pltpu.VMEM((steps, nb, 4, rb, m), jnp.bfloat16),
             pltpu.SemaphoreType.DMA((steps, nb)),
-            pltpu.SemaphoreType.DMA((steps, nb, 2 * GROUP)),
+            pltpu.SemaphoreType.DMA((steps, nb, 4)),
             pltpu.SemaphoreType.DMA((steps, nb, 2 * side)),
             pltpu.SemaphoreType.DMA((steps, nb, 2)),
-            pltpu.SemaphoreType.DMA((steps,)),
+            pltpu.SemaphoreType.DMA((7,)),
+            pltpu.SemaphoreType.DMA((steps, 2)),
         ],
         compiler_params=pltpu.CompilerParams(collective_id=0, has_side_effects=True),
-    )(delay_near, delay_far, incident, current_prev, current_prev2)
-    return blocks.transpose(0, 2, 4, 1, 3).reshape(steps, 2 * m, r)
+    )(
+        delay_near,
+        delay_far,
+        incident.transpose(0, 2, 1).reshape(steps, nb, rb, m),
+        current_prev.T.reshape(rows),
+        current_prev2.T.reshape(rows),
+    )
+    return blocks.reshape(steps, r, 2 * m).transpose(0, 2, 1)
 
 
 def solution(mesh):

time: 172 us -> 114 us (0.66)
  Pallas kernels: 161 us -> 111 us
  local copies, waits for them, and re-layouts: 10.7 us -> 2.67 us
    pallas_call x1, Pallas kernels: 161 us -> 111 us  [per_device(): pl.pallas_call(functools.partial(kernel, steps, nz, side), out_shape=jax....]
    transpose x1 -> x0, local copies, waits for them, and re-layouts: 3.03 us -> none  [per_device(): return blocks.transpose(0, 2, 4, 1, 3).reshape(steps, 2 * m, r)]
    unnamed x5 -> x1, local copies, waits for them, and re-layouts: 5.37 us -> 2.67 us
    reshape x1 -> x0, local copies, waits for them, and re-layouts: 2.33 us -> none  [per_device(): return blocks.transpose(0, 2, 4, 1, 3).reshape(steps, 2 * m, r)]
where the time goes in v2:
time: 114 us
  Pallas kernels  111 us (97%)
  local copies, waits for them, and re-layouts  2.67 us (2%)
    pallas_call x1, Pallas kernels, per_device(): pl.pallas_call(functools.partial(kernel, steps, nz, side), out_shape=jax....  111 us
    unnamed x1, local copies, waits for them, and re-layouts  2.67 us

profile of v2, /device:TPU:37, one launch (start us, length us, event | category | flops | bytes accessed | tf_op | source)
XLA Modules:
  0.0 113.6 jit_solution(15479210632779715692)
XLA Ops:
  0.0 110.9 %shard_map.55 = bf16[4,12,16,1024]{3,2,1,0:T(8,128)(2,1)} custom-call(bf16[512,1024]{1,0:T(8,128)(2,1)} %near_ref.1, bf16[512,1024]{1,0:T(8,128)(2,1)} %far_ref.1, bf16[4,12,16,512]{3,2,1,0:T(8,128)(2,1)} %bitcast.13, bf16[12,16,1024]{2,1,0:T(8,128)(2,1)} %bitcast.14, bf16[12,16,1024]{2,1,0:T(8,128)(2,1)} %bitcast.15), custom_call_target="tpu_custom_call" | custom-call | tf_op jit(solution)/shard_map/pallas_call | solution.py:309
  110.9 2.7 %copy.7 = bf16[4,1024,192]{1,2,0:T(8,128)(2,1)} copy(bf16[4,1024,192]{1,2,0:T(8,128)(2,1)} %bitcast.12) | data formatting | bytes 3145728

commit v3 on v2

--- a/solution.py
+++ b/solution.py
@@ -9,9 +9,11 @@
 from jax.sharding import PartitionSpec as P
 
 BATCHES = 12
-TOGETHER = 2
+TOGETHER = 1
 NEAR, FAR = 2, 6
-SKEW = 3
+SKEW = 2
+VMEM = 60 * 1024 * 1024
+LEAD = 1
 MESH = pl.DeviceIdType.MESH
 
 
@@ -61,13 +63,15 @@
     is_source = both(dx == 0, dy == 0)
     sibling = (z, chip * 2 + 1 - core)
 
-    def in_plane(kx, ky):
+    far_first = sorted(range(1, side), key=lambda k: -min(k, side - k))
+
+    def in_plane(kx, ky, which):
         tx = lax.rem(x + kx, side)
         ty = lax.rem(y + ky, side)
-        return (z, (tx * side + ty) * 2 + core)
-
-    peers = [in_plane(k, 0) for k in range(1, side)]
-    peers += [in_plane(0, k) for k in range(1, side)]
+        return (z, (tx * side + ty) * 2 + which)
+
+    peers = [in_plane(k, 0, c) for k in far_first for c in range(2)]
+    peers += [in_plane(0, k, c) for k in far_first for c in range(2)]
     peers += [sibling]
     reach = sorted({k % nz for k in (-FAR, -2, -1, 1, 2, FAR)} - {0})
     peers += [(lax.rem(z + k, nz), src) for k in reach]
@@ -135,46 +139,46 @@
             device_id=sibling, device_id_type=MESH,
         ).wait_recv()
 
-    def second_level(b):
+    def place(b):
         odd = lax.rem(b, 2)
-        across = jnp.where(odd == 0, dy, dx) == 0
-        return across, [in_plane(k * odd, k * (1 - odd)) for k in range(1, side)]
-
-    def first_level(b):
+        along, across = jnp.where(odd == 0, dx, dy), jnp.where(odd == 0, dy, dx)
+        return odd, along == 0, across == 0
+
+    def sweep(start, copies):
+        for copy in copies:
+            copy.start() if start else copy.wait_send()
+
+    def relay(t, b, start):
+        odd, no_along, no_across = place(b)
+
+        @pl.when(no_across)
+        def _():
+            sweep(start, [
+                down(t, b, k, in_plane(k * odd, k * (1 - odd), core)) for k in far_first
+            ])
+
+        @pl.when(both(no_across, jnp.logical_not(no_along)))
+        def _():
+            sweep(start, [
+                down(t, b, side + k, in_plane(k * odd, k * (1 - odd), 1 - core))
+                for k in far_first
+            ])
+
+        @pl.when(no_along | no_across)
+        def _():
+            sweep(start, [down(t, b, 0, sibling)])
+
+    def source(t, b, start):
         odd = lax.rem(b, 2)
-        return [in_plane(k * (1 - odd), k * odd) for k in range(1, side)]
-
-    def relay(t, b, start):
-        across, targets = second_level(b)
-
-        @pl.when(across)
-        def _():
-            for k, target in enumerate(targets):
-                copy = down(t, b, 1 + k, target)
-                copy.start() if start else copy.wait_send()
-
-        copy = down(t, b, 0, sibling)
-        copy.start() if start else copy.wait_send()
-
-    def source(t, b, start):
-        for k, target in enumerate(first_level(b)):
-            copy = down(t, b, side + k, target)
-            copy.start() if start else copy.wait_send()
+        sweep(start, [
+            down(t, b, side + k, in_plane(k * (1 - odd), k * odd, core)) for k in far_first
+        ])
 
     def take_own(t, b):
         @pl.when(jnp.logical_not(is_source))
         def _():
             wait_block(t, b, core)
             relay(t, b, True)
-
-    def ahead(t, b):
-        @pl.when(t > 0)
-        def _():
-            take_own(t - 1, b)
-
-        @pl.when(lax.rem(b, k) == k - 1)
-        def _():
-            multiply(t, b // k)
 
     def multiply(t, group):
         mine = pl.ds(group * k, k)
@@ -229,7 +233,9 @@
             source(t, b, True)
             relay(t, b, True)
 
-    skew = jnp.where(is_leaf, 0, jnp.where(is_root, nb, SKEW))
+    passes = both(jnp.logical_not(is_source), (dx == 0) | (dy == 0))
+    lead = jnp.where(passes, LEAD, 0)
+    skew = jnp.where(both(passes, is_joint), SKEW, 0)
 
     def out_copies(t):
         return [
@@ -241,11 +247,17 @@
 
     def step(t, carry):
         def turn(j, carry):
-            @pl.when(j < nb)
+            @pl.when(both(t > 0, j < nb))
             def _():
-                ahead(t, j)
-
-            @pl.when(both(j >= skew, j - skew < nb))
+                take_own(t - 1, j)
+
+            at = j - lead
+
+            @pl.when(both(at >= 0, at < nb, lax.rem(at, k) == k - 1))
+            def _():
+                multiply(t, at // k)
+
+            @pl.when(both(jnp.logical_not(is_leaf), j >= skew, j - skew < nb))
             def _():
                 behind(t, j - skew)
 
@@ -327,7 +339,9 @@
             pltpu.SemaphoreType.DMA((7,)),
             pltpu.SemaphoreType.DMA((steps, 2)),
         ],
-        compiler_params=pltpu.CompilerParams(collective_id=0, has_side_effects=True),
+        compiler_params=pltpu.CompilerParams(
+            collective_id=0, has_side_effects=True, vmem_limit_bytes=VMEM
+        ),
     )(
         delay_near,
         delay_far,

time: 114 us -> 106 us (0.930)
  the two profiles are of different devices: /device:TPU:37 before, /device:TPU:67 now
where the time goes in v3:
time: 106 us
  Pallas kernels  103 us (97%)
  local copies, waits for them, and re-layouts  2.67 us (3%)
    pallas_call x1, Pallas kernels, per_device(): pl.pallas_call(functools.partial(kernel, steps, nz, side), out_shape=jax....  103 us
    unnamed x1, local copies, waits for them, and re-layouts  2.67 us

profile of v3, /device:TPU:67, one launch (start us, length us, event | category | flops | bytes accessed | tf_op | source)
XLA Modules:
  0.0 105.7 jit_solution(4259015574256722093)
XLA Ops:
  0.0 103.1 %shard_map.55 = bf16[4,12,16,1024]{3,2,1,0:T(8,128)(2,1)} custom-call(bf16[512,1024]{1,0:T(8,128)(2,1)} %near_ref.1, bf16[512,1024]{1,0:T(8,128)(2,1)} %far_ref.1, bf16[4,12,16,512]{3,2,1,0:T(8,128)(2,1)} %bitcast.13, bf16[12,16,1024]{2,1,0:T(8,128)(2,1)} %bitcast.14, bf16[12,16,1024]{2,1,0:T(8,128)(2,1)} %bitcast.15), custom_call_target="tpu_custom_call" | custom-call | tf_op jit(solution)/shard_map/pallas_call | solution.py:321
  103.1 2.7 %copy.7 = bf16[4,1024,192]{1,2,0:T(8,128)(2,1)} copy(bf16[4,1024,192]{1,2,0:T(8,128)(2,1)} %bitcast.12) | data formatting | bytes 3145728

commit v4 on v3

--- a/solution.py
+++ b/solution.py
@@ -65,13 +65,13 @@
 
     far_first = sorted(range(1, side), key=lambda k: -min(k, side - k))
 
-    def in_plane(kx, ky, which):
-        tx = lax.rem(x + kx, side)
-        ty = lax.rem(y + ky, side)
-        return (z, (tx * side + ty) * 2 + which)
-
-    peers = [in_plane(k, 0, c) for k in far_first for c in range(2)]
-    peers += [in_plane(0, k, c) for k in far_first for c in range(2)]
+    on_x = {k: (lax.rem(x + k, side) * side + y) * 2 for k in far_first}
+    on_y = {k: (x * side + lax.rem(y + k, side)) * 2 for k in far_first}
+
+    def in_plane(swap, k, which):
+        return (z, jnp.where(swap == 0, on_x[k], on_y[k]) + which)
+
+    peers = [(z, on_axis[k] + c) for on_axis in (on_x, on_y) for k in far_first for c in range(2)]
     peers += [sibling]
     reach = sorted({k % nz for k in (-FAR, -2, -1, 1, 2, FAR)} - {0})
     peers += [(lax.rem(z + k, nz), src) for k in reach]
@@ -94,21 +94,20 @@
 
     k = TOGETHER
 
-    def dot(index, group, ref, half):
-        rows = cur[index, pl.ds(group * k, k), half].reshape(k * rb, m)
+    def dot(index, first, count, ref, half):
+        rows = cur[index, pl.ds(first, count), half].reshape(count * rb, m)
         cols = pl.ds(pl.multiple_of(half * m, m), m)
         field = lax.dot_general(
             rows, ref[:, cols], (((1,), (1,)), ((), ())), preferred_element_type=jnp.float32
         )
-        return field.reshape(k, rb, m)
-
-    def lagged(index, group):
-        lag[pl.ds(group * k, k)] = dot(index, group, far, 0) + dot(index, group, far, 1)
+        return field.reshape(count, rb, m)
+
+    def lagged(index):
+        lag[...] = dot(index, 0, nb, far, 0) + dot(index, 0, nb, far, 1)
 
     for load in loads[:3]:
         load.wait()
-    for group in range(nb // k):
-        lagged(0, group)
+    lagged(0)
     for load in loads[3:]:
         load.wait()
 
@@ -154,13 +153,13 @@
         @pl.when(no_across)
         def _():
             sweep(start, [
-                down(t, b, k, in_plane(k * odd, k * (1 - odd), core)) for k in far_first
+                down(t, b, k, in_plane(1 - odd, k, core)) for k in far_first
             ])
 
         @pl.when(both(no_across, jnp.logical_not(no_along)))
         def _():
             sweep(start, [
-                down(t, b, side + k, in_plane(k * odd, k * (1 - odd), 1 - core))
+                down(t, b, side + k, in_plane(1 - odd, k, 1 - core))
                 for k in far_first
             ])
 
@@ -171,7 +170,7 @@
     def source(t, b, start):
         odd = lax.rem(b, 2)
         sweep(start, [
-            down(t, b, side + k, in_plane(k * (1 - odd), k * odd, core)) for k in far_first
+            down(t, b, side + k, in_plane(odd, k, core)) for k in far_first
         ])
 
     def take_own(t, b):
@@ -182,14 +181,12 @@
 
     def multiply(t, group):
         mine = pl.ds(group * k, k)
-        total = lag[mine] + dot(t + 1, group, near, core)
-
         @pl.when(t > 0)
         def _():
             for i in range(k):
                 wait_block(t - 1, group * k + i, 1 - core)
 
-        total = total + dot(t + 1, group, near, 1 - core)
+        total = lag[mine] + dot(t + 1, group * k, k, near, 0) + dot(t + 1, group * k, k, near, 1)
 
         @pl.when(is_leaf)
         def _():
@@ -272,11 +269,7 @@
 
         @pl.when(t < steps - 1)
         def _():
-            def refill(group, carry):
-                lagged(t + 1, group)
-                return carry
-
-            lax.fori_loop(0, nb // k, refill, 0)
+            lagged(t + 1)
 
         return carry
 

time: 106 us -> 106 us (level)
  the two profiles are of different devices: /device:TPU:67 before, /device:TPU:35 now
where the time goes in v4:
time: 106 us
  Pallas kernels  103 us (97%)
  local copies, waits for them, and re-layouts  2.67 us (3%)
    pallas_call x1, Pallas kernels, per_device(): pl.pallas_call(functools.partial(kernel, steps, nz, side), out_shape=jax....  103 us
    unnamed x1, local copies, waits for them, and re-layouts  2.67 us

profile of v4, /device:TPU:35, one launch (start us, length us, event | category | flops | bytes accessed | tf_op | source)
XLA Modules:
  0.0 105.6 jit_solution(8682433604364596468)
XLA Ops:
  0.0 102.9 %shard_map.55 = bf16[4,12,16,1024]{3,2,1,0:T(8,128)(2,1)} custom-call(bf16[512,1024]{1,0:T(8,128)(2,1)} %near_ref.1, bf16[512,1024]{1,0:T(8,128)(2,1)} %far_ref.1, bf16[4,12,16,512]{3,2,1,0:T(8,128)(2,1)} %bitcast.13, bf16[12,16,1024]{2,1,0:T(8,128)(2,1)} %bitcast.14, bf16[12,16,1024]{2,1,0:T(8,128)(2,1)} %bitcast.15), custom_call_target="tpu_custom_call" | custom-call | tf_op jit(solution)/shard_map/pallas_call | solution.py:314
  102.9 2.7 %copy.7 = bf16[4,1024,192]{1,2,0:T(8,128)(2,1)} copy(bf16[4,1024,192]{1,2,0:T(8,128)(2,1)} %bitcast.12) | data formatting | bytes 3145728
